TPU v7x, 32 devices: a whole 2x2x4 slice. The times are simulated.
32 devices in a mesh: energy: 8 (over y, x, core), elem: 4 (over z).
Axes of the slice: x: 2, y: 2, z: 4, core: 2. Of those that a mesh axis runs over, the one named last changes fastest.
Arguments:
- g_lesser: bfloat16 [2, 512, 2048], P(None, 'energy', 'elem'), may hold values from -6 to 6
- g_greater: bfloat16 [2, 512, 2048], P(None, 'energy', 'elem'), may hold values from -6 to 6
- send_rows: int32 [4, 8, 4, 32], P('elem'), may hold values from 0 to 63, as said below
- partner_slot: int32 [2048], P('elem'), may hold values from 0 to 127, as said below
Outputs:
- polarization_lesser: bfloat16 [2, 512, 2048], P(None, 'energy', 'elem')
- polarization_greater: bfloat16 [2, 512, 2048], P(None, 'energy', 'elem')
Inputs may be any that keep to these rules, and one draw needn't show every extreme that they name: partner is an involution on the elements that keeps the element piece n. The groups fall into two halves of 2 groups; for a sending group b and element piece n, send_rows[b, n, a, :] lists 32 distinct rows when a lies in b's half (b itself included) and zeros otherwise; every row of that piece of the sender appears exactly once over all receivers of its half. `partner_slot`: every slot named points into a receiving group's half and to a slot that carries a row; the 64 elements of one element piece of a group name 64 distinct slots.
All inputs are finite; a program needn't handle non-finite values.
Results may differ from a plain program's by a relative error of at most 0.001.
Values may be sent and summed in bfloat16 or wider, within the bound.
No kernel may reach another device: no remote copies, remote signals or barrier semaphores. Data moves between devices by JAX's collectives and lax.ppermute only.
A program may use at most 64 MiB of HBM per device.

v0:
```python
from functools import partial
import math
import jax
import jax.numpy as jnp
from jax import lax
from jax.sharding import PartitionSpec as P


def factor_pair(length):
    divisor = math.isqrt(length)
    while length % divisor:
        divisor -= 1
    return divisor


def phase_tables(rows_count, cols_count, modulus, inverse):
    sign_factor = 1.0 if inverse else -1.0
    left_index = jnp.arange(rows_count, dtype=jnp.int32)
    right_index = jnp.arange(cols_count, dtype=jnp.int32)
    phases = (left_index[:, None] * right_index[None, :] % modulus).astype(jnp.float32) * (
        2.0 * math.pi / modulus
    )
    return (jnp.cos(phases), sign_factor * jnp.sin(phases))


def transform(real_part, imag_part, inverse):
    signals, length, width = real_part.shape
    first_size = factor_pair(length)
    second_size = length // first_size
    cos_first, sin_first = phase_tables(first_size, first_size, first_size, inverse)
    cos_twist, sin_twist = phase_tables(first_size, second_size, length, inverse)
    cos_second, sin_second = phase_tables(second_size, second_size, second_size, inverse)
    product = partial(jnp.einsum, precision=lax.Precision.HIGHEST)
    real_grid = real_part.reshape(signals, first_size, second_size, width)
    imag_grid = imag_part.reshape(signals, first_size, second_size, width)
    inner_re = product("ka,sabe->skbe", cos_first, real_grid) - product(
        "ka,sabe->skbe", sin_first, imag_grid
    )
    inner_im = product("ka,sabe->skbe", cos_first, imag_grid) + product(
        "ka,sabe->skbe", sin_first, real_grid
    )
    twist_cos = cos_twist[None, :, :, None]
    twist_sin = sin_twist[None, :, :, None]
    twist_re = inner_re * twist_cos - inner_im * twist_sin
    twist_im = inner_re * twist_sin + inner_im * twist_cos
    outer_re = product("qb,skbe->sqke", cos_second, twist_re) - product(
        "qb,skbe->sqke", sin_second, twist_im
    )
    outer_im = product("qb,skbe->sqke", cos_second, twist_im) + product(
        "qb,skbe->sqke", sin_second, twist_re
    )
    return (outer_re.reshape(signals, length, width), outer_im.reshape(signals, length, width))


def reverse_energy(values):
    return jnp.roll(jnp.flip(values, axis=1), 1, axis=1)


def shards(g_lesser, g_greater, send_rows, partner_slot):
    piece_index = lax.axis_index("energy")
    energy_count = lax.axis_size("energy")
    group_rows = partner_slot.shape[0]
    elem_dev = group_rows // energy_count
    own_lesser, own_greater = (
        lax.all_to_all(g_lesser, "energy", split_axis=2, concat_axis=1, tiled=True),
        lax.all_to_all(g_greater, "energy", split_axis=2, concat_axis=1, tiled=True),
    )
    own_rows = jnp.stack([own_lesser, own_greater])
    partner_columns = lax.dynamic_slice_in_dim(partner_slot, piece_index * elem_dev, elem_dev, 0)
    chosen_rows = lax.dynamic_index_in_dim(send_rows[0], piece_index, 0, keepdims=False).reshape(-1)
    outgoing = jnp.take(own_rows, chosen_rows, axis=3)
    incoming = lax.all_to_all(outgoing, "elem", split_axis=3, concat_axis=3, tiled=True)
    partner_rows = jnp.take(incoming, partner_columns, axis=3)
    signals = jnp.concatenate([own_rows, partner_rows], 0).astype(jnp.float32)
    spec_re, spec_im = transform(signals[:, 0], signals[:, 1], False)
    near_re = spec_re[:2]
    near_im = spec_im[:2]
    far_re = reverse_energy(jnp.stack([spec_re[3], spec_re[2]]))
    far_im = reverse_energy(jnp.stack([spec_im[3], spec_im[2]]))
    prod_re = near_re * far_re - near_im * far_im
    prod_im = near_re * far_im + near_im * far_re
    back_re, back_im = transform(prod_re, prod_im, True)
    length = back_re.shape[1]
    factor = 1.0 / (length * math.sqrt(length))
    result = jnp.stack([factor * back_im, -factor * back_re], 1).astype(jnp.bfloat16)
    lesser_out, greater_out = (
        lax.all_to_all(result[0], "energy", split_axis=1, concat_axis=2, tiled=True),
        lax.all_to_all(result[1], "energy", split_axis=1, concat_axis=2, tiled=True),
    )
    return (lesser_out, greater_out)


def solution(mesh):
    in_specs = (
        P(None, "energy", "elem"),
        P(None, "energy", "elem"),
        P("elem", None, None, None),
        P("elem"),
    )
    out_specs = (P(None, "energy", "elem"), P(None, "energy", "elem"))
    return jax.shard_map(shards, mesh=mesh, in_specs=in_specs, out_specs=out_specs, check_vma=False)
```

profile of v0, /device:TPU:0, one launch (start us, length us, event | category | flops | bytes accessed | tf_op | source)
XLA Modules:
  0.0 93.1 jit_solution(4972418240594326676)
XLA Ops:
  0.6 1.1 %copy.86 = bf16[2,64,512]{1,0,2:T(2,128)(2,1)S(1)} copy(bf16[2,64,512]{2,1,0:T(8,128)(2,1)} %param.4) | data formatting | bytes 262144 | tf_op args[0]
  1.7 0.9 reshape.175
  2.6 5.3 %all-to-all-start = ((bf16[8,2,4096]{2,1,0:T(2,128)(2,1)}), bf16[8,2,4096]{2,1,0:T(2,128)(2,1)S(1)}, u32[]{:S(2)}, u32[]{:S(2)}) async-start(bf16[8,2,4096]{2,1,0:T(2,128)(2,1)} %reshape.175), calls=%async_computation | async-start | bytes 262144 | tf_op jit(solution)/shard_map/all_to_all | solution.py:65
  8.3 0.9 reshape.173
  9.2 4.3 %all-to-all-done = bf16[8,2,4096]{2,1,0:T(2,128)(2,1)S(1)} async-done(((bf16[8,2,4096]{2,1,0:T(2,128)(2,1)}), bf16[8,2,4096]{2,1,0:T(2,128)(2,1)S(1)}, u32[]{:S(2)}, u32[]{:S(2)}) %all-to-all-start) | async-done | bytes 131104 | tf_op jit(solution)/shard_map/all_to_all | solution.py:65
  13.5 3.4 %all-to-all-start.1 = ((bf16[8,2,4096]{2,1,0:T(2,128)(2,1)}), bf16[8,2,4096]{2,1,0:T(2,128)(2,1)S(1)}, u32[]{:S(2)}, u32[]{:S(2)}) async-start(bf16[8,2,4096]{2,1,0:T(2,128)(2,1)} %reshape.173), calls=%async_computation.1 | async-start | bytes 262144 | tf_op jit(solution)/shard_map/all_to_all | solution.py:66
  16.9 0.2 reshape.176
  17.1 0.2 copy.182
  17.3 0.2 stack.21
  17.6 4.7 %all-to-all-done.1 = bf16[8,2,4096]{2,1,0:T(2,128)(2,1)S(1)} async-done(((bf16[8,2,4096]{2,1,0:T(2,128)(2,1)}), bf16[8,2,4096]{2,1,0:T(2,128)(2,1)S(1)}, u32[]{:S(2)}, u32[]{:S(2)}) %all-to-all-start.1) | async-done | bytes 131104 | tf_op jit(solution)/shard_map/all_to_all | solution.py:66
  22.3 0.2 reshape.174
  22.5 0.2 copy.181
  22.7 0.2 stack.22
  23.1 0.4 pad_maximum_fusion.4
  23.4 1.7 %gather_fusion = bf16[128,2,2,512]{3,2,1,0:T(2,128)(2,1)S(1)} fusion(bf16[2,2,512,64]{2,1,3,0:T(2,128)(2,1)S(1)} %pad_maximum_fusion.4, s32[1024]{0:T(1024)S(1)} %pad_clamp_fusion.1), kind=kCustom, calls=%fused_computation | custom fusion | bytes 1049088 | tf_op jit(solution)/shard_map/jit(_take)/gather | solution.py:71
  25.1 1.4 %fusion.22 = bf16[2,2,512,128]{2,1,0,3:T(2,128)(2,1)} fusion(bf16[128,2,2,512]{3,2,1,0:T(2,128)(2,1)S(1)} %gather_fusion, pred[128]{0:T(512)(128)(4,1)S(1)} %compare_and_fusion), kind=kLoop, calls=%fused_computation.49 | loop fusion | flops 262144 | bytes 1048704 | tf_op jit(solution)/shard_map/jit(_take)/select_n | solution.py:71
  26.5 4.9 %all-to-all-start.2 = ((bf16[2,2,512,128]{2,1,0,3:T(2,128)(2,1)}), bf16[2,2,512,128]{2,1,0,3:T(2,128)(2,1)S(1)}, u32[]{:S(2)}, u32[]{:S(2)}) async-start(bf16[2,2,512,128]{2,1,0,3:T(2,128)(2,1)} %fusion.22), calls=%async_computation.2 | async-start | bytes 1048576 | tf_op jit(solution)/shard_map/all_to_all | solution.py:72
  31.4 0.8 compare_and_fusion.1
  32.6 13.1 %all-to-all-done.2 = bf16[2,2,512,128]{2,1,0,3:T(2,128)(2,1)S(1)} async-done(((bf16[2,2,512,128]{2,1,0,3:T(2,128)(2,1)}), bf16[2,2,512,128]{2,1,0,3:T(2,128)(2,1)S(1)}, u32[]{:S(2)}, u32[]{:S(2)}) %all-to-all-start.2) | async-done | bytes 524320 | tf_op jit(solution)/shard_map/all_to_all | solution.py:72
  45.7 0.4 copy.92
  46.0 1.1 %gather_fusion.1 = bf16[64,2,2,512]{3,2,1,0:T(2,128)(2,1)S(1)} fusion(bf16[2,2,512,128]{2,1,3,0:T(2,128)(2,1)S(1)} %copy.92, s32[1024]{0:T(1024)S(1)} %pad_clamp_fusion), kind=kCustom, calls=%fused_computation.1 | custom fusion | bytes 524544 | tf_op jit(solution)/shard_map/jit(_take)/gather | solution.py:73
  47.1 0.3 fusion.44
  47.5 0.7 pad_maximum_fusion.2
  48.2 0.7 fusion.180
  48.9 0.5 copy.95
  49.5 0.7 copy.97
  50.2 0.6 fusion.35
  50.8 0.6 fusion.39
  51.4 0.6 fusion.3
  52.1 0.9 multiply_add_fusion
  53.0 1.4 %fusion.12 = f32[4,16,64,32]{2,3,1,0:T(8,128)S(1)} fusion(f32[4,16,32,64]{3,1,2,0:T(8,128)S(1)} %get-tuple-element.4), kind=kOutput, calls=%fused_computation.25 | convolution fusion | flops 50345984 | bytes 1048576 | tf_op jit(solution)/shard_map/qb,skbe->sqke/dot_general | solution.py:49
  54.4 1.4 %fusion.16 = f32[4,16,64,32]{2,3,1,0:T(8,128)S(1)} fusion(f32[4,16,32,64]{3,1,2,0:T(8,128)S(1)} %get-tuple-element.5), kind=kOutput, calls=%fused_computation.29 | convolution fusion | flops 50345984 | bytes 1048576 | tf_op jit(solution)/shard_map/qb,skbe->sqke/dot_general | solution.py:46
  55.8 1.4 %fusion.1 = f32[4,32,16,64]{3,1,2,0:T(8,128)S(1)} fusion(f32[4,16,64,32]{2,3,1,0:T(8,128)S(1)} %fusion.16, f32[4,16,32,64]{3,1,2,0:T(8,128)S(1)} %get-tuple-element.4), kind=kOutput, calls=%fused_computation.5 | convolution fusion | flops 50478080 | bytes 1572864 | tf_op jit(solution)/shard_map/qb,skbe->sqke/dot_general | solution.py:46
  57.2 1.0 %copy-done.1 = f32[4,32,16,64]{3,1,2,0:T(8,128)} copy-done((f32[4,32,16,64]{3,1,2,0:T(8,128)}, f32[4,32,16,64]{3,1,2,0:T(8,128)S(1)}, u32[]{:S(2)}) %copy-start.1) | copy-done | bytes 524312
  58.2 1.4 %fusion = f32[4,32,16,64]{3,1,2,0:T(8,128)S(1)} fusion(f32[4,16,64,32]{2,3,1,0:T(8,128)S(1)} %fusion.12, f32[4,16,32,64]{3,1,2,0:T(8,128)S(1)} %get-tuple-element.5), kind=kOutput, calls=%fused_computation.3 | convolution fusion | flops 50478080 | bytes 1572864 | tf_op jit(solution)/shard_map/qb,skbe->sqke/dot_general | solution.py:49
  59.6 1.0 %copy-done.2 = f32[4,32,16,64]{3,1,2,0:T(8,128)} copy-done((f32[4,32,16,64]{3,1,2,0:T(8,128)}, f32[4,32,16,64]{3,1,2,0:T(8,128)S(1)}, u32[]{:S(2)}) %copy-start.2) | copy-done | bytes 524312
  60.8 0.9 slice-done
  61.7 0.3 copy.103
  62.2 0.7 slice.80
  63.1 0.9 slice-done.1
  64.0 0.3 copy.108
  64.5 0.9 slice.89
  65.5 0.3 fusion.20
  65.7 0.9 fusion.33
  66.6 0.9 fusion.29
  67.5 0.9 fusion.7
  68.4 1.1 %multiply_subtract_fusion.1 = (f32[2,16,32,64]{3,1,2,0:T(8,128)S(1)}, f32[2,16,32,64]{3,1,2,0:T(8,128)S(1)}) fusion(f32[2,16,32,64]{3,1,2,0:T(8,128)S(1)} %fusion.7, f32[16,32]{0,1:T(8,128)S(1)} %get-tuple-element.19, f32[16,32]{0,1:T(8,128)S(1)} %fusion.90, f32[2,32,64,16]{2,3,1,0:T(8,128)S(1)} %fusion.29, f32[2,16,32,64]{3,2,1,0:T(8,128)S(1)} %get-tuple-element.6), kind=kOutput, calls=%fused_computation.47 | convolution fusion | flops 13045248 | bytes 1314816 | tf_op jit(solution)/shard_map/ka,sabe->skbe/dot_general | solution.py:39
  69.5 0.8 fusion.23
  70.3 0.8 fusion.27
  71.0 0.8 fusion.10
  71.8 0.8 fusion.11
  73.0 0.3 copy.183
  73.2 0.9 reshape.179
  74.1 3.4 %all-to-all-start.4 = ((bf16[8,2,4096]{2,1,0:T(2,128)(2,1)}), bf16[8,2,4096]{2,1,0:T(2,128)(2,1)S(1)}, u32[]{:S(2)}, u32[]{:S(2)}) async-start(bf16[8,2,4096]{2,1,0:T(2,128)(2,1)} %reshape.179), calls=%async_computation.4 | async-start | bytes 262144 | tf_op jit(solution)/shard_map/all_to_all | solution.py:88
  77.5 0.3 copy.184
  77.8 0.9 reshape.177
  78.7 4.3 %all-to-all-done.4 = bf16[8,2,4096]{2,1,0:T(2,128)(2,1)S(1)} async-done(((bf16[8,2,4096]{2,1,0:T(2,128)(2,1)}), bf16[8,2,4096]{2,1,0:T(2,128)(2,1)S(1)}, u32[]{:S(2)}, u32[]{:S(2)}) %all-to-all-start.4) | async-done | bytes 131104 | tf_op jit(solution)/shard_map/all_to_all | solution.py:88
  83.0 3.4 %all-to-all-start.3 = ((bf16[8,2,4096]{2,1,0:T(2,128)(2,1)}), bf16[8,2,4096]{2,1,0:T(2,128)(2,1)S(1)}, u32[]{:S(2)}, u32[]{:S(2)}) async-start(bf16[8,2,4096]{2,1,0:T(2,128)(2,1)} %reshape.177), calls=%async_computation.3 | async-start | bytes 262144 | tf_op jit(solution)/shard_map/all_to_all | solution.py:87
  86.4 0.2 reshape.180
  86.6 0.2 copy.179
  86.8 0.9 all_to_all.65
  87.6 4.2 %all-to-all-done.3 = bf16[8,2,4096]{2,1,0:T(2,128)(2,1)S(1)} async-done(((bf16[8,2,4096]{2,1,0:T(2,128)(2,1)}), bf16[8,2,4096]{2,1,0:T(2,128)(2,1)S(1)}, u32[]{:S(2)}, u32[]{:S(2)}) %all-to-all-start.3) | async-done | bytes 131104 | tf_op jit(solution)/shard_map/all_to_all | solution.py:87
  91.8 0.2 reshape.178
  92.2 0.9 all_to_all.61
  (36 shorter events, 2.5 us)
Async XLA Ops:
  0.6 7.3 %copy-start = (s32[1,8,4,32]{3,2,1,0:T(4,128)S(1)}, s32[1,8,4,32]{3,2,1,0:T(4,128)}, u32[]{:S(2)}) copy-start(s32[1,8,4,32]{3,2,1,0:T(4,128)} %param.6) | copy-start | bytes 12292
  2.6 5.5 %copy-start.3 = (bf16[2,64,512]{2,1,0:T(8,128)(2,1)S(1)}, bf16[2,64,512]{2,1,0:T(8,128)(2,1)}, u32[]{:S(2)}) copy-start(bf16[2,64,512]{2,1,0:T(8,128)(2,1)} %param.5) | copy-start | bytes 393220
  2.6 10.8 %all-to-all-start = ((bf16[8,2,4096]{2,1,0:T(2,128)(2,1)}), bf16[8,2,4096]{2,1,0:T(2,128)(2,1)S(1)}, u32[]{:S(2)}, u32[]{:S(2)}) async-start(bf16[8,2,4096]{2,1,0:T(2,128)(2,1)} %reshape.175), calls=%async_computation | async-start | bytes 262144 | tf_op jit(solution)/shard_map/all_to_all | solution.py:65
  13.5 8.8 %all-to-all-start.1 = ((bf16[8,2,4096]{2,1,0:T(2,128)(2,1)}), bf16[8,2,4096]{2,1,0:T(2,128)(2,1)S(1)}, u32[]{:S(2)}, u32[]{:S(2)}) async-start(bf16[8,2,4096]{2,1,0:T(2,128)(2,1)} %reshape.173), calls=%async_computation.1 | async-start | bytes 262144 | tf_op jit(solution)/shard_map/all_to_all | solution.py:66
  26.5 19.2 %all-to-all-start.2 = ((bf16[2,2,512,128]{2,1,0,3:T(2,128)(2,1)}), bf16[2,2,512,128]{2,1,0,3:T(2,128)(2,1)S(1)}, u32[]{:S(2)}, u32[]{:S(2)}) async-start(bf16[2,2,512,128]{2,1,0,3:T(2,128)(2,1)} %fusion.22), calls=%async_computation.2 | async-start | bytes 1048576 | tf_op jit(solution)/shard_map/all_to_all | solution.py:72
  57.2 1.0 %copy-start.1 = (f32[4,32,16,64]{3,1,2,0:T(8,128)}, f32[4,32,16,64]{3,1,2,0:T(8,128)S(1)}, u32[]{:S(2)}) copy-start(f32[4,32,16,64]{3,1,2,0:T(8,128)S(1)} %fusion.1) | copy-start | bytes 1572868
  59.6 1.0 %copy-start.2 = (f32[4,32,16,64]{3,1,2,0:T(8,128)}, f32[4,32,16,64]{3,1,2,0:T(8,128)S(1)}, u32[]{:S(2)}) copy-start(f32[4,32,16,64]{3,1,2,0:T(8,128)S(1)} %fusion) | copy-start | bytes 1572868
  60.6 1.0 %slice-start = ((f32[4,32,16,64]{3,1,2,0:T(8,128)}), f32[2,32,16,64]{3,1,2,0:T(8,128)S(1)}, s32[]{:S(2)}) async-start(f32[4,32,16,64]{3,1,2,0:T(8,128)} %copy-done.1), calls=%async_computation.5 | async-start | bytes 1048576 | tf_op jit(solution)/shard_map/slice | solution.py:76
  62.9 1.0 %slice-start.1 = ((f32[4,32,16,64]{3,1,2,0:T(8,128)}), f32[2,32,16,64]{3,1,2,0:T(8,128)S(1)}, s32[]{:S(2)}) async-start(f32[4,32,16,64]{3,1,2,0:T(8,128)} %copy-done.2), calls=%async_computation.6 | async-start | bytes 1048576 | tf_op jit(solution)/shard_map/slice | solution.py:77
  74.1 8.8 %all-to-all-start.4 = ((bf16[8,2,4096]{2,1,0:T(2,128)(2,1)}), bf16[8,2,4096]{2,1,0:T(2,128)(2,1)S(1)}, u32[]{:S(2)}, u32[]{:S(2)}) async-start(bf16[8,2,4096]{2,1,0:T(2,128)(2,1)} %reshape.179), calls=%async_computation.4 | async-start | bytes 262144 | tf_op jit(solution)/shard_map/all_to_all | solution.py:88
  83.0 8.8 %all-to-all-start.3 = ((bf16[8,2,4096]{2,1,0:T(2,128)(2,1)}), bf16[8,2,4096]{2,1,0:T(2,128)(2,1)S(1)}, u32[]{:S(2)}, u32[]{:S(2)}) async-start(bf16[8,2,4096]{2,1,0:T(2,128)(2,1)} %reshape.177), calls=%async_computation.3 | async-start | bytes 262144 | tf_op jit(solution)/shard_map/all_to_all | solution.py:87
where the time goes:
time: 93.8 us; the launch traced here: 93.1 us
  waiting for transfers between devices  30.5 us (33%)
  local copies, waits for them, and re-layouts  21.7 us (23%)
  starting transfers between devices  20.3 us (22%)
  matrix products  15.2 us (16%)
  other arithmetic  4.33 us (5%)
  between operations  1.15 us (1%)
    all_to_all x1, waiting for transfers between devices, shards(): lax.all_to_all(outgoing, 'elem', split_axis=3, concat_axis=3, tiled=True)  13.1 us
    unnamed x18, local copies, waits for them, and re-layouts  7.64 us
    all_to_all x1, starting transfers between devices, shards(): lax.all_to_all(g_lesser, 'energy', split_axis=2, concat_axis=1, tiled=True)  5.3 us
    all_to_all x1, starting transfers between devices, shards(): lax.all_to_all(outgoing, 'elem', split_axis=3, concat_axis=3, tiled=True)  4.87 us
    all_to_all x1, waiting for transfers between devices, shards(): lax.all_to_all(g_greater, 'energy', split_axis=2, concat_axis=1, tiled=True)  4.68 us
    all_to_all x1, waiting for transfers between devices, shards(): lax.all_to_all(result[1], 'energy', split_axis=1, concat_axis=2, tiled=True)  4.29 us
    all_to_all x1, waiting for transfers between devices, shards(): lax.all_to_all(g_lesser, 'energy', split_axis=2, concat_axis=1, tiled=True)  4.26 us
    all_to_all x1, waiting for transfers between devices, shards(): lax.all_to_all(result[0], 'energy', split_axis=1, concat_axis=2, tiled=True)  4.19 us
  transfers between devices with their start and end apart: 5, of which 5 were waited for; matrix products, arithmetic and copies ran while one was open for 5% of the time, Pallas kernels for 0%

commit v1 on v0

--- a/solution.py
+++ b/solution.py
@@ -85,7 +85,15 @@
     result = jnp.stack([factor * back_im, -factor * back_re], 1).astype(jnp.bfloat16)
     lesser_out, greater_out = (
         lax.all_to_all(result[0], "energy", split_axis=1, concat_axis=2, tiled=True),
-        lax.all_to_all(result[1], "energy", split_axis=1, concat_axis=2, tiled=True),
+        jnp.concatenate(
+            lax.all_to_all(
+                jnp.stack(jnp.split(result[1], lax.axis_size("energy"), 1), axis=0),
+                axis_name="energy",
+                split_axis=0,
+                concat_axis=0,
+            ),
+            2,
+        ),
     )
     return (lesser_out, greater_out)
 

time: 93.8 us -> 93.8 us (level)
    reshape x0 -> x2, local copies, waits for them, and re-layouts: none -> 1.04 us  [shards(): jnp.concatenate(lax.all_to_all(jnp.stack(jnp.split(result[1], lax.axis_si...]
    all_to_all x2 -> x0, local copies, waits for them, and re-layouts: 1.04 us -> none  [shards(): lax.all_to_all(result[1], 'energy', split_axis=1, concat_axis=2, tiled=True)]
    unnamed x18 -> x25, local copies, waits for them, and re-layouts: 7.64 us -> 7.71 us
where the time goes in v1:
time: 93.8 us; the launch traced here: 93.1 us
  waiting for transfers between devices  30.6 us (33%)
  local copies, waits for them, and re-layouts  21.5 us (23%)
  starting transfers between devices  20.3 us (22%)
  matrix products  15.2 us (16%)
  other arithmetic  4.33 us (5%)
  between operations  1.19 us (1%)
    all_to_all x1, waiting for transfers between devices, shards(): lax.all_to_all(outgoing, 'elem', split_axis=3, concat_axis=3, tiled=True)  13.1 us
    unnamed x25, local copies, waits for them, and re-layouts  7.71 us
    all_to_all x1, starting transfers between devices, shards(): lax.all_to_all(g_lesser, 'energy', split_axis=2, concat_axis=1, tiled=True)  5.3 us
    all_to_all x1, starting transfers between devices, shards(): lax.all_to_all(outgoing, 'elem', split_axis=3, concat_axis=3, tiled=True)  4.87 us
    all_to_all x1, waiting for transfers between devices, shards(): lax.all_to_all(g_greater, 'energy', split_axis=2, concat_axis=1, tiled=True)  4.68 us
    all_to_all x1, waiting for transfers between devices, shards(): lax.all_to_all(result[0], 'energy', split_axis=1, concat_axis=2, tiled=True)  4.45 us
    all_to_all x1, waiting for transfers between devices, shards(): lax.all_to_all(g_lesser, 'energy', split_axis=2, concat_axis=1, tiled=True)  4.26 us
    all_to_all x1, waiting for transfers between devices, shards(): lax.all_to_all(jnp.stack(jnp.split(result[1], lax.axis_size('energy'), 1)...  4.19 us
  transfers between devices with their start and end apart: 5, of which 5 were waited for; matrix products, arithmetic and copies ran while one was open for 5% of the time, Pallas kernels for 0%

profile of v1, /device:TPU:0, one launch (start us, length us, event | category | flops | bytes accessed | tf_op | source)
XLA Modules:
  0.0 93.1 jit_solution(12157943108908006727)
XLA Ops:
  0.6 1.1 %copy.91 = bf16[2,64,512]{1,0,2:T(2,128)(2,1)S(1)} copy(bf16[2,64,512]{2,1,0:T(8,128)(2,1)} %param.4) | data formatting | bytes 262144 | tf_op args[0]
  1.7 0.9 reshape.183
  2.6 5.3 %all-to-all-start = ((bf16[8,2,4096]{2,1,0:T(2,128)(2,1)}), bf16[8,2,4096]{2,1,0:T(2,128)(2,1)S(1)}, u32[]{:S(2)}, u32[]{:S(2)}) async-start(bf16[8,2,4096]{2,1,0:T(2,128)(2,1)} %reshape.183), calls=%async_computation | async-start | bytes 262144 | tf_op jit(solution)/shard_map/all_to_all | solution.py:65
  8.3 0.9 reshape.181
  9.2 4.3 %all-to-all-done = bf16[8,2,4096]{2,1,0:T(2,128)(2,1)S(1)} async-done(((bf16[8,2,4096]{2,1,0:T(2,128)(2,1)}), bf16[8,2,4096]{2,1,0:T(2,128)(2,1)S(1)}, u32[]{:S(2)}, u32[]{:S(2)}) %all-to-all-start) | async-done | bytes 131104 | tf_op jit(solution)/shard_map/all_to_all | solution.py:65
  13.5 3.4 %all-to-all-start.1 = ((bf16[8,2,4096]{2,1,0:T(2,128)(2,1)}), bf16[8,2,4096]{2,1,0:T(2,128)(2,1)S(1)}, u32[]{:S(2)}, u32[]{:S(2)}) async-start(bf16[8,2,4096]{2,1,0:T(2,128)(2,1)} %reshape.181), calls=%async_computation.1 | async-start | bytes 262144 | tf_op jit(solution)/shard_map/all_to_all | solution.py:66
  16.9 0.2 reshape.184
  17.1 0.2 copy.175
  17.3 0.2 stack.48
  17.6 4.7 %all-to-all-done.1 = bf16[8,2,4096]{2,1,0:T(2,128)(2,1)S(1)} async-done(((bf16[8,2,4096]{2,1,0:T(2,128)(2,1)}), bf16[8,2,4096]{2,1,0:T(2,128)(2,1)S(1)}, u32[]{:S(2)}, u32[]{:S(2)}) %all-to-all-start.1) | async-done | bytes 131104 | tf_op jit(solution)/shard_map/all_to_all | solution.py:66
  22.3 0.2 reshape.182
  22.5 0.2 copy.174
  22.7 0.2 stack.49
  23.1 0.4 pad_maximum_fusion.4
  23.4 1.7 %gather_fusion = bf16[128,2,2,512]{3,2,1,0:T(2,128)(2,1)S(1)} fusion(bf16[2,2,512,64]{2,1,3,0:T(2,128)(2,1)S(1)} %pad_maximum_fusion.4, s32[1024]{0:T(1024)S(1)} %pad_clamp_fusion.1), kind=kCustom, calls=%fused_computation | custom fusion | bytes 1049088 | tf_op jit(solution)/shard_map/jit(_take)/gather | solution.py:71
  25.1 1.4 %fusion.22 = bf16[2,2,512,128]{2,1,0,3:T(2,128)(2,1)} fusion(bf16[128,2,2,512]{3,2,1,0:T(2,128)(2,1)S(1)} %gather_fusion, pred[128]{0:T(512)(128)(4,1)S(1)} %compare_and_fusion), kind=kLoop, calls=%fused_computation.49 | loop fusion | flops 262144 | bytes 1048704 | tf_op jit(solution)/shard_map/jit(_take)/select_n | solution.py:71
  26.5 4.9 %all-to-all-start.2 = ((bf16[2,2,512,128]{2,1,0,3:T(2,128)(2,1)}), bf16[2,2,512,128]{2,1,0,3:T(2,128)(2,1)S(1)}, u32[]{:S(2)}, u32[]{:S(2)}) async-start(bf16[2,2,512,128]{2,1,0,3:T(2,128)(2,1)} %fusion.22), calls=%async_computation.2 | async-start | bytes 1048576 | tf_op jit(solution)/shard_map/all_to_all | solution.py:72
  31.4 0.8 compare_and_fusion.1
  32.6 13.1 %all-to-all-done.2 = bf16[2,2,512,128]{2,1,0,3:T(2,128)(2,1)S(1)} async-done(((bf16[2,2,512,128]{2,1,0,3:T(2,128)(2,1)}), bf16[2,2,512,128]{2,1,0,3:T(2,128)(2,1)S(1)}, u32[]{:S(2)}, u32[]{:S(2)}) %all-to-all-start.2) | async-done | bytes 524320 | tf_op jit(solution)/shard_map/all_to_all | solution.py:72
  45.7 0.4 copy.97
  46.0 1.1 %gather_fusion.1 = bf16[64,2,2,512]{3,2,1,0:T(2,128)(2,1)S(1)} fusion(bf16[2,2,512,128]{2,1,3,0:T(2,128)(2,1)S(1)} %copy.97, s32[1024]{0:T(1024)S(1)} %pad_clamp_fusion), kind=kCustom, calls=%fused_computation.1 | custom fusion | bytes 524544 | tf_op jit(solution)/shard_map/jit(_take)/gather | solution.py:73
  47.1 0.3 fusion.44
  47.5 0.7 pad_maximum_fusion.2
  48.2 0.7 fusion.188
  48.9 0.5 copy.100
  49.5 0.7 copy.102
  50.2 0.6 fusion.35
  50.8 0.6 fusion.39
  51.4 0.6 fusion.3
  52.1 0.9 multiply_add_fusion
  53.0 1.4 %fusion.12 = f32[4,16,64,32]{2,3,1,0:T(8,128)S(1)} fusion(f32[4,16,32,64]{3,1,2,0:T(8,128)S(1)} %get-tuple-element.4), kind=kOutput, calls=%fused_computation.25 | convolution fusion | flops 50345984 | bytes 1048576 | tf_op jit(solution)/shard_map/qb,skbe->sqke/dot_general | solution.py:49
  54.4 1.4 %fusion.16 = f32[4,16,64,32]{2,3,1,0:T(8,128)S(1)} fusion(f32[4,16,32,64]{3,1,2,0:T(8,128)S(1)} %get-tuple-element.5), kind=kOutput, calls=%fused_computation.29 | convolution fusion | flops 50345984 | bytes 1048576 | tf_op jit(solution)/shard_map/qb,skbe->sqke/dot_general | solution.py:46
  55.8 1.4 %fusion.1 = f32[4,32,16,64]{3,1,2,0:T(8,128)S(1)} fusion(f32[4,16,64,32]{2,3,1,0:T(8,128)S(1)} %fusion.16, f32[4,16,32,64]{3,1,2,0:T(8,128)S(1)} %get-tuple-element.4), kind=kOutput, calls=%fused_computation.5 | convolution fusion | flops 50478080 | bytes 1572864 | tf_op jit(solution)/shard_map/qb,skbe->sqke/dot_general | solution.py:46
  57.2 1.0 %copy-done.1 = f32[4,32,16,64]{3,1,2,0:T(8,128)} copy-done((f32[4,32,16,64]{3,1,2,0:T(8,128)}, f32[4,32,16,64]{3,1,2,0:T(8,128)S(1)}, u32[]{:S(2)}) %copy-start.1) | copy-done | bytes 524312
  58.2 1.4 %fusion = f32[4,32,16,64]{3,1,2,0:T(8,128)S(1)} fusion(f32[4,16,64,32]{2,3,1,0:T(8,128)S(1)} %fusion.12, f32[4,16,32,64]{3,1,2,0:T(8,128)S(1)} %get-tuple-element.5), kind=kOutput, calls=%fused_computation.3 | convolution fusion | flops 50478080 | bytes 1572864 | tf_op jit(solution)/shard_map/qb,skbe->sqke/dot_general | solution.py:49
  59.6 1.0 %copy-done.2 = f32[4,32,16,64]{3,1,2,0:T(8,128)} copy-done((f32[4,32,16,64]{3,1,2,0:T(8,128)}, f32[4,32,16,64]{3,1,2,0:T(8,128)S(1)}, u32[]{:S(2)}) %copy-start.2) | copy-done | bytes 524312
  60.8 0.9 slice-done
  61.7 0.3 copy.108
  62.2 0.7 slice.80
  63.1 0.9 slice-done.1
  64.0 0.3 copy.113
  64.5 0.9 slice.89
  65.5 0.3 fusion.20
  65.7 0.9 fusion.33
  66.6 0.9 fusion.29
  67.5 0.9 fusion.7
  68.4 1.1 %multiply_subtract_fusion.1 = (f32[2,16,32,64]{3,1,2,0:T(8,128)S(1)}, f32[2,16,32,64]{3,1,2,0:T(8,128)S(1)}) fusion(f32[2,16,32,64]{3,1,2,0:T(8,128)S(1)} %fusion.7, f32[16,32]{0,1:T(8,128)S(1)} %get-tuple-element.19, f32[16,32]{0,1:T(8,128)S(1)} %fusion.98, f32[2,32,64,16]{2,3,1,0:T(8,128)S(1)} %fusion.29, f32[2,16,32,64]{3,2,1,0:T(8,128)S(1)} %get-tuple-element.6), kind=kOutput, calls=%fused_computation.47 | convolution fusion | flops 13045248 | bytes 1314816 | tf_op jit(solution)/shard_map/ka,sabe->skbe/dot_general | solution.py:39
  69.5 0.8 fusion.23
  70.3 0.8 fusion.27
  71.0 0.8 fusion.10
  71.8 0.8 fusion.11
  73.0 0.3 copy.176
  73.2 0.9 reshape.185
  74.1 3.4 %all-to-all-start.3 = ((bf16[8,2,4096]{2,1,0:T(2,128)(2,1)}), bf16[8,2,4096]{2,1,0:T(2,128)(2,1)S(1)}, u32[]{:S(2)}, u32[]{:S(2)}) async-start(bf16[8,2,4096]{2,1,0:T(2,128)(2,1)} %reshape.185), calls=%async_computation.3 | async-start | bytes 262144 | tf_op jit(solution)/shard_map/all_to_all | solution.py:87
  77.6 0.9 reshape.187
  78.5 4.4 %all-to-all-done.3 = bf16[8,2,4096]{2,1,0:T(2,128)(2,1)S(1)} async-done(((bf16[8,2,4096]{2,1,0:T(2,128)(2,1)}), bf16[8,2,4096]{2,1,0:T(2,128)(2,1)S(1)}, u32[]{:S(2)}, u32[]{:S(2)}) %all-to-all-start.3) | async-done | bytes 131104 | tf_op jit(solution)/shard_map/all_to_all | solution.py:87
  83.0 3.4 %all-to-all-start.4 = ((bf16[8,2,4096]{2,1,0:T(2,128)(2,1)}), bf16[8,2,4096]{2,1,0:T(2,128)(2,1)S(1)}, u32[]{:S(2)}, u32[]{:S(2)}) async-start(bf16[8,2,4096]{2,1,0:T(2,128)(2,1)} %reshape.187), calls=%async_computation.4 | async-start | bytes 262144 | tf_op jit(solution)/shard_map/all_to_all | solution.py:89
  86.4 0.2 reshape.186
  86.6 0.2 copy.127
  86.8 0.9 all_to_all.51
  87.6 4.2 %all-to-all-done.4 = bf16[8,2,4096]{2,1,0:T(2,128)(2,1)S(1)} async-done(((bf16[8,2,4096]{2,1,0:T(2,128)(2,1)}), bf16[8,2,4096]{2,1,0:T(2,128)(2,1)S(1)}, u32[]{:S(2)}, u32[]{:S(2)}) %all-to-all-start.4) | async-done | bytes 131104 | tf_op jit(solution)/shard_map/all_to_all | solution.py:89
  91.8 0.2 reshape.188
  92.0 0.2 copy.128
  92.2 0.9 reshape.157
  (43 shorter events, 2.4 us)
Async XLA Ops:
  0.6 7.3 %copy-start = (s32[1,8,4,32]{3,2,1,0:T(4,128)S(1)}, s32[1,8,4,32]{3,2,1,0:T(4,128)}, u32[]{:S(2)}) copy-start(s32[1,8,4,32]{3,2,1,0:T(4,128)} %param.6) | copy-start | bytes 12292
  2.6 5.5 %copy-start.3 = (bf16[2,64,512]{2,1,0:T(8,128)(2,1)S(1)}, bf16[2,64,512]{2,1,0:T(8,128)(2,1)}, u32[]{:S(2)}) copy-start(bf16[2,64,512]{2,1,0:T(8,128)(2,1)} %param.5) | copy-start | bytes 393220
  2.6 10.8 %all-to-all-start = ((bf16[8,2,4096]{2,1,0:T(2,128)(2,1)}), bf16[8,2,4096]{2,1,0:T(2,128)(2,1)S(1)}, u32[]{:S(2)}, u32[]{:S(2)}) async-start(bf16[8,2,4096]{2,1,0:T(2,128)(2,1)} %reshape.183), calls=%async_computation | async-start | bytes 262144 | tf_op jit(solution)/shard_map/all_to_all | solution.py:65
  13.5 8.8 %all-to-all-start.1 = ((bf16[8,2,4096]{2,1,0:T(2,128)(2,1)}), bf16[8,2,4096]{2,1,0:T(2,128)(2,1)S(1)}, u32[]{:S(2)}, u32[]{:S(2)}) async-start(bf16[8,2,4096]{2,1,0:T(2,128)(2,1)} %reshape.181), calls=%async_computation.1 | async-start | bytes 262144 | tf_op jit(solution)/shard_map/all_to_all | solution.py:66
  26.5 19.2 %all-to-all-start.2 = ((bf16[2,2,512,128]{2,1,0,3:T(2,128)(2,1)}), bf16[2,2,512,128]{2,1,0,3:T(2,128)(2,1)S(1)}, u32[]{:S(2)}, u32[]{:S(2)}) async-start(bf16[2,2,512,128]{2,1,0,3:T(2,128)(2,1)} %fusion.22), calls=%async_computation.2 | async-start | bytes 1048576 | tf_op jit(solution)/shard_map/all_to_all | solution.py:72
  57.2 1.0 %copy-start.1 = (f32[4,32,16,64]{3,1,2,0:T(8,128)}, f32[4,32,16,64]{3,1,2,0:T(8,128)S(1)}, u32[]{:S(2)}) copy-start(f32[4,32,16,64]{3,1,2,0:T(8,128)S(1)} %fusion.1) | copy-start | bytes 1572868
  59.6 1.0 %copy-start.2 = (f32[4,32,16,64]{3,1,2,0:T(8,128)}, f32[4,32,16,64]{3,1,2,0:T(8,128)S(1)}, u32[]{:S(2)}) copy-start(f32[4,32,16,64]{3,1,2,0:T(8,128)S(1)} %fusion) | copy-start | bytes 1572868
  60.6 1.0 %slice-start = ((f32[4,32,16,64]{3,1,2,0:T(8,128)}), f32[2,32,16,64]{3,1,2,0:T(8,128)S(1)}, s32[]{:S(2)}) async-start(f32[4,32,16,64]{3,1,2,0:T(8,128)} %copy-done.1), calls=%async_computation.5 | async-start | bytes 1048576 | tf_op jit(solution)/shard_map/slice | solution.py:76
  62.9 1.0 %slice-start.1 = ((f32[4,32,16,64]{3,1,2,0:T(8,128)}), f32[2,32,16,64]{3,1,2,0:T(8,128)S(1)}, s32[]{:S(2)}) async-start(f32[4,32,16,64]{3,1,2,0:T(8,128)} %copy-done.2), calls=%async_computation.6 | async-start | bytes 1048576 | tf_op jit(solution)/shard_map/slice | solution.py:77
  74.1 8.8 %all-to-all-start.3 = ((bf16[8,2,4096]{2,1,0:T(2,128)(2,1)}), bf16[8,2,4096]{2,1,0:T(2,128)(2,1)S(1)}, u32[]{:S(2)}, u32[]{:S(2)}) async-start(bf16[8,2,4096]{2,1,0:T(2,128)(2,1)} %reshape.185), calls=%async_computation.3 | async-start | bytes 262144 | tf_op jit(solution)/shard_map/all_to_all | solution.py:87
  83.0 8.8 %all-to-all-start.4 = ((bf16[8,2,4096]{2,1,0:T(2,128)(2,1)}), bf16[8,2,4096]{2,1,0:T(2,128)(2,1)S(1)}, u32[]{:S(2)}, u32[]{:S(2)}) async-start(bf16[8,2,4096]{2,1,0:T(2,128)(2,1)} %reshape.187), calls=%async_computation.4 | async-start | bytes 262144 | tf_op jit(solution)/shard_map/all_to_all | solution.py:89
